TPU v7x, 256 devices: a whole 4x4x8 slice. The times are simulated.
256 devices in a mesh: sect: 4 (over y), pass: 16 (over z, core), qry: 4 (over x).
Axes of the slice: x: 4, y: 4, z: 8, core: 2. Of those that a mesh axis runs over, the one named last changes fastest.
Arguments:
- query_emb: bfloat16 [8192, 4096], P(('sect', 'qry')), may hold values from -0.2 to 0.2
- passage_emb: bfloat16 [16384, 4096], P(('sect', 'pass')), may hold values from -0.2 to 0.2
- block_ids: int32 [32, 64], P(('sect', 'qry')), may hold values from 0 to 255, as said below
- positives: int32 [8192], P(('sect', 'qry')), may hold values from 0 to 16383, as said below
Outputs:
- query_grad: bfloat16 [8192, 4096], P(('sect', 'qry'), 'pass')
- pool_grad: bfloat16 [16384, 4096], P(('sect', 'pass', 'qry'))
Inputs may be any that keep to these rules, and one draw needn't show every extreme that they name: `block_ids`: each row names 64 different passage blocks. `positives`: the positive passage of a query lies in a block that its query block's row of block_ids names.
All inputs are finite; a program needn't handle non-finite values.
Results may differ from a plain program's by a relative error of at most 0.015.
Values may be sent and summed in bfloat16 or wider, within the bound.
A program may use at most 128 MiB of HBM per device.

v0:
```python
import jax
import jax.numpy as jnp
from jax import lax
from jax.sharding import PartitionSpec as P

QBR = 256
PBR = 64
LOGIT_SCALE = 50.0
NEG_FILL = -1e30


def inner_rows(first_operand, second_operand):
    return lax.dot_general(
        first_operand, second_operand, (((1,), (1,)), ((), ())), preferred_element_type=jnp.float32
    )


def inner_cols(first_operand, second_operand):
    return lax.dot_general(
        first_operand, second_operand, (((0,), (0,)), ((), ())), preferred_element_type=jnp.float32
    )


def body(query_emb, passage_emb, block_ids, positives):
    section_count = lax.axis_size("sect")
    shard_count = lax.axis_size("pass")
    shard_index = lax.axis_index("pass")
    query_rows, embed_width = query_emb.shape
    passage_rows = passage_emb.shape[0]
    query_blocks = query_rows // QBR
    per_piece = passage_rows // PBR
    local_count = section_count * per_piece
    candidates = section_count * passage_rows
    gathered = lax.all_gather(passage_emb, "sect", axis=0, tiled=True)
    local_ids = jnp.arange(local_count, dtype=jnp.int32)
    global_blocks = (
        local_ids // per_piece * shard_count + shard_index
    ) * per_piece + local_ids % per_piece
    allowed = jnp.any(block_ids[:, :, None] == global_blocks[None, None, :], axis=1)
    allowed_rows = jnp.broadcast_to(
        allowed[:, None, :, None], (query_blocks, QBR, local_count, PBR)
    )
    allowed_rows = allowed_rows.reshape(query_rows, candidates)
    global_rows = (
        global_blocks[:, None] * PBR + jnp.arange(PBR, dtype=jnp.int32)[None, :]
    ).reshape(candidates)
    target = (positives[:, None] == global_rows[None, :]).astype(jnp.float32)
    scores = LOGIT_SCALE * inner_rows(query_emb, gathered)
    local_top = jnp.max(jnp.where(allowed_rows, scores, NEG_FILL), axis=1)
    row_top = lax.pmax(local_top, "pass")
    exp_terms = jnp.where(allowed_rows, jnp.exp(scores - row_top[:, None]), 0.0)
    row_sum = lax.psum(jnp.sum(exp_terms, axis=1), "pass")
    score_grad = (LOGIT_SCALE * (exp_terms / row_sum[:, None] - target)).astype(jnp.bfloat16)
    query_part = jnp.dot(score_grad, gathered, preferred_element_type=jnp.float32)
    pool_part = inner_cols(score_grad, query_emb)
    query_part = query_part.astype(jnp.bfloat16)
    pool_part = pool_part.astype(jnp.bfloat16)
    query_grad = (
        lax.psum_scatter(query_part, "pass", scatter_dimension=1, tiled=True)
        .astype(jnp.float32)
        .astype(jnp.bfloat16)
    )
    pool_grad = (
        lax.psum_scatter(pool_part, ("sect", "qry"), scatter_dimension=0, tiled=True)
        .astype(jnp.float32)
        .astype(jnp.bfloat16)
    )
    return (query_grad, pool_grad)


def solution(mesh):
    return jax.shard_map(
        body,
        mesh=mesh,
        in_specs=(
            P(("sect", "qry"), None),
            P(("sect", "pass"), None),
            P(("sect", "qry"), None),
            P(("sect", "qry")),
        ),
        out_specs=(P(("sect", "qry"), "pass"), P(("sect", "pass", "qry"), None)),
        check_vma=False,
    )
```

profile of v0, /device:TPU:2, one launch (start us, length us, event | category | flops | bytes accessed | tf_op | source)
XLA Modules:
  0.0 329.6 jit_solution(13325460295013534195)
XLA Ops:
  7.2 0.0 copy-start
  7.2 0.0 all-gather.2.cloned.1.call-start
  7.2 0.7 all-gather.2.cloned.1.call-update
  7.9 0.0 reduce-scatter.3.cloned.1.call-start
  8.0 0.1 iota_add_fusion
  8.0 0.1 add.81
  8.1 0.0 copy-done
  8.1 0.2 compare_reduce_fusion
  8.3 0.3 broadcast_in_dim.8
  8.7 2.4 reshape.76
  11.1 87.4 %all-gather.2.cloned.1.call-done = bf16[1024,4096]{1,0:T(8,128)(2,1)} async-done(((bf16[256,4096]{1,0:T(8,128)(2,1)}), bf16[1024,4096]{1,0:T(8,128)(2,1)}) %all-gather.2.cloned.1.call-update) | async-done | bytes 8388624 | tf_op jit(solution)/shard_map/all_gather | solution.py:34
  98.4 8.4 %select_reduce_fusion = (f32[512]{0:T(512)S(1)}, f32[512,1024]{1,0:T(8,128)S(1)}) fusion(pred[512,1024]{1,0:T(32,128)(4,1)S(1)} %reshape.76, bf16[512,4096]{1,0:T(8,128)(2,1)} %param.4, bf16[1024,4096]{1,0:T(8,128)(2,1)} %all-gather.2.cloned.1.call-done), kind=kOutput, calls=%fused_computation.4 | convolution fusion | flops 4296539648 | bytes 15206400 | tf_op jit(solution)/shard_map/dot_general | solution.py:13
  106.8 0.0 copy-start.1
  106.9 26.1 %pmax.7 = f32[512]{0:T(512)S(1)} all-reduce(f32[512]{0:T(512)S(1)} %get-tuple-element.2), channel_id=1, replica_groups=mesh['sect'=4,'pass'=16,'qry'=4] {'pass'}, use_global_device_ids=true, to_apply=%region_2.3 | all-reduce | flops 512 | bytes 4096 | tf_op jit(solution)/shard_map/pmax | solution.py:50
  133.0 0.7 fusion
  133.7 23.5 %psum.7 = f32[512]{0:T(512)S(1)} all-reduce(f32[512]{0:T(512)S(1)} %fusion), channel_id=1, replica_groups=mesh['sect'=4,'pass'=16,'qry'=4] {'pass'}, use_global_device_ids=true, to_apply=%region_4.5 | all-reduce | flops 512 | bytes 4096 | tf_op jit(solution)/shard_map/psum | solution.py:52
  157.2 0.0 copy-done.1
  157.2 10.3 %convolution_convert_fusion.1 = bf16[512,4096]{1,0:T(8,128)(2,1)} fusion(bf16[1024,4096]{1,0:T(8,128)(2,1)} %all-gather.2.cloned.1.call-done, pred[512,1024]{1,0:T(32,128)(4,1)S(1)} %reshape.76, f32[512,1024]{1,0:T(8,128)S(1)} %get-tuple-element.3, s32[1024]{0:T(1024)S(1)} %add.81, f32[512]{0:T(512)S(1)} %psum.7, f32[512]{0:T(512)S(1)} %pmax.7, ...), kind=kOutput, calls=%fused_computation.1 | convolution fusion | flops 4301783040 | bytes 15214592 | tf_op jit(solution)/shard_map/dot_general | solution.py:54
  167.5 0.0 reduce-scatter.3.cloned.1.call-update
  167.5 0.0 reduce-scatter.5.cloned.1.call-start
  167.6 9.5 %convolution_convert_fusion = bf16[1024,4096]{1,0:T(8,128)(2,1)} fusion(bf16[512,4096]{1,0:T(8,128)(2,1)} %param.4, pred[512,1024]{1,0:T(32,128)(4,1)S(1)} %reshape.76, f32[512,1024]{1,0:T(8,128)S(1)} %get-tuple-element.3, s32[1024]{0:T(1024)S(1)} %add.81, f32[512]{0:T(512)S(1)} %psum.7, f32[512]{0:T(512)S(1)} %pmax.7, s32[512]{0:T(512)S(1)} %copy-done.1), kind=kOutput, calls=%fused_computation | convolution fusion | flops 4303880192 | bytes 15214592 | tf_op jit(solution)/shard_map/dot_general | solution.py:19
  177.1 0.0 reduce-scatter.5.cloned.1.call-update
  177.1 52.2 %reduce-scatter.3.cloned.1.call-done = bf16[512,256]{1,0:T(8,128)(2,1)} async-done(((bf16[512,4096]{1,0:T(8,128)(2,1)}), bf16[512,256]{1,0:T(8,128)(2,1)}) %reduce-scatter.3.cloned.1.call-update) | async-done | bytes 262160 | tf_op jit(solution)/shard_map/reduce_scatter | solution.py:59
  229.3 93.7 %reduce-scatter.5.cloned.1.call-done = bf16[64,4096]{1,0:T(8,128)(2,1)} async-done(((bf16[1024,4096]{1,0:T(8,128)(2,1)}), bf16[64,4096]{1,0:T(8,128)(2,1)}) %reduce-scatter.5.cloned.1.call-update) | async-done | bytes 524304 | tf_op jit(solution)/shard_map/reduce_scatter | solution.py:64
  (1 shorter events, 0.0 us)
Async XLA Ops:
  7.2 1.0 copy-start
  7.2 91.2 %all-gather.2.cloned.1.call-start = ((), (), s32[]{:S(2)}) async-start(), calls=%async_computation.2 | async-start | bytes 10485760 | tf_op jit(solution)/shard_map/all_gather | solution.py:34
  7.9 221.4 %reduce-scatter.3.cloned.1.call-start = ((), (), s32[]{:S(2)}) async-start(), calls=%async_computation.3 | async-start | bytes 4456448 | tf_op jit(solution)/shard_map/reduce_scatter | solution.py:59
  106.8 50.4 %copy-start.1 = (s32[512]{0:T(512)S(1)}, s32[512]{0:T(512)}, u32[]{:S(2)}) copy-start(s32[512]{0:T(512)} %param.7) | copy-start | bytes 6148
  167.5 155.5 %reduce-scatter.5.cloned.1.call-start = ((), (), s32[]{:S(2)}) async-start(), calls=%async_computation.4 | async-start | bytes 8912896 | tf_op jit(solution)/shard_map/reduce_scatter | solution.py:64
Sparse Core Ops, SparseCore 0:
  9.8 88.5 all-gather.1
  167.6 61.6 reduce-scatter.2
  233.6 89.3 reduce-scatter.4
where the time goes:
time: 330 us
  waiting for transfers between devices  234 us (71%)
  blocking collectives  49.7 us (15%)
  matrix products  28.2 us (9%)
  between operations  13.8 us (4%)
    reduce_scatter x1, waiting for transfers between devices, body(): lax.psum_scatter(pool_part, ('sect', 'qry'), scatter_dimension=0, tiled=T...  93.7 us
    all_gather x1, waiting for transfers between devices, body(): gathered = lax.all_gather(passage_emb, 'sect', axis=0, tiled=True)  87.4 us
    reduce_scatter x1, waiting for transfers between devices, body(): lax.psum_scatter(query_part, 'pass', scatter_dimension=1, tiled=True)  52.2 us
    pmax x1, blocking collectives, body(): row_top = lax.pmax(local_top, 'pass')  26.1 us
    psum x1, blocking collectives, body(): row_sum = lax.psum(jnp.sum(exp_terms, axis=1), 'pass')  23.5 us
    dot_general x1, matrix products, body(): jnp.dot(score_grad, gathered, preferred_element_type=jnp.float32)  10.3 us
    dot_general x1, matrix products, inner_cols(): lax.dot_general(first_operand, second_operand, (((0,), (0,)), ((), ())),...  9.5 us
    dot_general x1, matrix products, inner_rows(): lax.dot_general(first_operand, second_operand, (((1,), (1,)), ((), ())),...  8.42 us
  transfers between devices with their start and end apart: 3, of which 3 were waited for; matrix products, arithmetic and copies ran while one was open for 4% of the time, Pallas kernels for 0%

commit v1 on v0

--- a/solution.py
+++ b/solution.py
@@ -31,7 +31,9 @@
     per_piece = passage_rows // PBR
     local_count = section_count * per_piece
     candidates = section_count * passage_rows
-    gathered = lax.all_gather(passage_emb, "sect", axis=0, tiled=True)
+    gathered = jnp.concatenate(
+        lax.all_to_all(jnp.stack([passage_emb] * lax.axis_size("sect")), "sect", 0, 0), axis=0
+    )
     local_ids = jnp.arange(local_count, dtype=jnp.int32)
     global_blocks = (
         local_ids // per_piece * shard_count + shard_index

time: 330 us -> 344 us (1.042)
  local copies, waits for them, and re-layouts: 2.82 us -> 8.67 us
  starting transfers between devices: 0.12 us -> 5.87 us
    all_to_all x0 -> x1, waiting for transfers between devices: none -> 90.9 us  [body(): lax.all_to_all(jnp.stack([passage_emb] * lax.axis_size('sect')), 'sect',...]
    all_gather x1 -> x0, waiting for transfers between devices: 87.4 us -> none  [body(): gathered = lax.all_gather(passage_emb, 'sect', axis=0, tiled=True)]
    another operation x0 -> x1, local copies, waits for them, and re-layouts: none -> 5.86 us  [body(): jnp.stack([passage_emb] * lax.axis_size('sect'))]
    all_to_all x0 -> x1, starting transfers between devices: none -> 5.78 us  [body(): lax.all_to_all(jnp.stack([passage_emb] * lax.axis_size('sect')), 'sect',...]
where the time goes in v1:
time: 344 us
  waiting for transfers between devices  235 us (68%)
  blocking collectives  51.5 us (15%)
  matrix products  28.2 us (8%)
  between operations  14.1 us (4%)
  local copies, waits for them, and re-layouts  8.67 us (3%)
  starting transfers between devices  5.87 us (2%)
    reduce_scatter x1, waiting for transfers between devices, body(): lax.psum_scatter(pool_part, ('sect', 'qry'), scatter_dimension=0, tiled=T...  93.6 us
    all_to_all x1, waiting for transfers between devices, body(): lax.all_to_all(jnp.stack([passage_emb] * lax.axis_size('sect')), 'sect',...  90.9 us
    reduce_scatter x1, waiting for transfers between devices, body(): lax.psum_scatter(query_part, 'pass', scatter_dimension=1, tiled=True)  50.3 us
    pmax x1, blocking collectives, body(): row_top = lax.pmax(local_top, 'pass')  28 us
    psum x1, blocking collectives, body(): row_sum = lax.psum(jnp.sum(exp_terms, axis=1), 'pass')  23.5 us
    dot_general x1, matrix products, body(): jnp.dot(score_grad, gathered, preferred_element_type=jnp.float32)  10.3 us
    dot_general x1, matrix products, inner_cols(): lax.dot_general(first_operand, second_operand, (((0,), (0,)), ((), ())),...  9.49 us
    dot_general x1, matrix products, inner_rows(): lax.dot_general(first_operand, second_operand, (((1,), (1,)), ((), ())),...  8.42 us
  transfers between devices with their start and end apart: 3, of which 3 were waited for; matrix products, arithmetic and copies ran while one was open for 4% of the time, Pallas kernels for 0%

profile of v1, /device:TPU:2, one launch (start us, length us, event | category | flops | bytes accessed | tf_op | source)
XLA Modules:
  0.0 344.2 jit_solution(7399749634560542439)
XLA Ops:
  7.2 5.9 %stack.2 = bf16[4,256,4096]{2,1,0:T(8,128)(2,1)} broadcast(bf16[256,4096]{1,0:T(8,128)(2,1)} %param.5), dimensions={1,2} | broadcast | bytes 10485760 | tf_op jit(solution)/shard_map/stack | solution.py:35
  13.0 0.0 copy-start
  13.0 5.8 %all-to-all-start = ((bf16[4,256,4096]{2,1,0:T(8,128)(2,1)}), bf16[4,256,4096]{2,1,0:T(8,128)(2,1)}, u32[]{:S(2)}, u32[]{:S(2)}) async-start(bf16[4,256,4096]{2,1,0:T(8,128)(2,1)} %stack.2), calls=%async_computation | async-start | bytes 16777216 | tf_op jit(solution)/shard_map/all_to_all | solution.py:35
  18.8 0.0 reduce-scatter.3.cloned.1.call-start
  18.9 0.0 copy-done
  18.9 0.2 compare_reduce_fusion
  19.1 0.3 broadcast_in_dim.8
  19.4 2.4 reshape.81
  21.8 0.1 iota_add_fusion
  21.9 0.1 add.81
  22.0 90.9 %all-to-all-done = bf16[4,256,4096]{2,1,0:T(8,128)(2,1)} async-done(((bf16[4,256,4096]{2,1,0:T(8,128)(2,1)}), bf16[4,256,4096]{2,1,0:T(8,128)(2,1)}, u32[]{:S(2)}, u32[]{:S(2)}) %all-to-all-start) | async-done | bytes 8388640 | tf_op jit(solution)/shard_map/all_to_all | solution.py:35
  112.9 8.4 %select_reduce_fusion = (f32[512]{0:T(512)S(1)}, f32[512,1024]{1,0:T(8,128)S(1)}) fusion(pred[512,1024]{1,0:T(32,128)(4,1)S(1)} %reshape.81, bf16[512,4096]{1,0:T(8,128)(2,1)} %param.4, bf16[1024,4096]{1,0:T(8,128)(2,1)} %bitcast), kind=kOutput, calls=%fused_computation.4 | convolution fusion | flops 4296539648 | bytes 15206400 | tf_op jit(solution)/shard_map/dot_general | solution.py:13
  121.3 0.0 copy-start.1
  121.3 28.0 %pmax.7 = f32[512]{0:T(512)S(1)} all-reduce(f32[512]{0:T(512)S(1)} %get-tuple-element.2), channel_id=1, replica_groups=mesh['sect'=4,'pass'=16,'qry'=4] {'pass'}, use_global_device_ids=true, to_apply=%region_2.3 | all-reduce | flops 512 | bytes 4096 | tf_op jit(solution)/shard_map/pmax | solution.py:52
  149.3 0.7 fusion
  150.0 23.5 %psum.7 = f32[512]{0:T(512)S(1)} all-reduce(f32[512]{0:T(512)S(1)} %fusion), channel_id=1, replica_groups=mesh['sect'=4,'pass'=16,'qry'=4] {'pass'}, use_global_device_ids=true, to_apply=%region_4.5 | all-reduce | flops 512 | bytes 4096 | tf_op jit(solution)/shard_map/psum | solution.py:54
  173.6 0.0 copy-done.1
  173.6 10.3 %convolution_convert_fusion.1 = bf16[512,4096]{1,0:T(8,128)(2,1)} fusion(bf16[1024,4096]{1,0:T(8,128)(2,1)} %bitcast, pred[512,1024]{1,0:T(32,128)(4,1)S(1)} %reshape.81, f32[512,1024]{1,0:T(8,128)S(1)} %get-tuple-element.3, s32[1024]{0:T(1024)S(1)} %add.81, f32[512]{0:T(512)S(1)} %psum.7, f32[512]{0:T(512)S(1)} %pmax.7, s32[512]{0:T(512)S(1)} %copy-done.1), kind=kOutput, calls=%fused_computation.1 | convolution fusion | flops 4301783040 | bytes 15214592 | tf_op jit(solution)/shard_map/dot_general | solution.py:56
  183.8 0.0 reduce-scatter.3.cloned.1.call-update
  183.8 0.0 reduce-scatter.5.cloned.1.call-start
  183.9 9.5 %convolution_convert_fusion = bf16[1024,4096]{1,0:T(8,128)(2,1)} fusion(bf16[512,4096]{1,0:T(8,128)(2,1)} %param.4, pred[512,1024]{1,0:T(32,128)(4,1)S(1)} %reshape.81, f32[512,1024]{1,0:T(8,128)S(1)} %get-tuple-element.3, s32[1024]{0:T(1024)S(1)} %add.81, f32[512]{0:T(512)S(1)} %psum.7, f32[512]{0:T(512)S(1)} %pmax.7, s32[512]{0:T(512)S(1)} %copy-done.1), kind=kOutput, calls=%fused_computation | convolution fusion | flops 4303880192 | bytes 15214592 | tf_op jit(solution)/shard_map/dot_general | solution.py:19
  193.4 0.0 reduce-scatter.5.cloned.1.call-update
  193.4 50.3 %reduce-scatter.3.cloned.1.call-done = bf16[512,256]{1,0:T(8,128)(2,1)} async-done(((bf16[512,4096]{1,0:T(8,128)(2,1)}), bf16[512,256]{1,0:T(8,128)(2,1)}) %reduce-scatter.3.cloned.1.call-update) | async-done | bytes 262160 | tf_op jit(solution)/shard_map/reduce_scatter | solution.py:61
  243.8 93.6 %reduce-scatter.5.cloned.1.call-done = bf16[64,4096]{1,0:T(8,128)(2,1)} async-done(((bf16[1024,4096]{1,0:T(8,128)(2,1)}), bf16[64,4096]{1,0:T(8,128)(2,1)}) %reduce-scatter.5.cloned.1.call-update) | async-done | bytes 524304 | tf_op jit(solution)/shard_map/reduce_scatter | solution.py:66
  (1 shorter events, 0.0 us)
Async XLA Ops:
  13.0 5.9 %copy-start = (s32[2,64]{1,0:T(2,128)S(1)}, s32[2,64]{1,0:T(2,128)}, u32[]{:S(2)}) copy-start(s32[2,64]{1,0:T(2,128)} %param.6) | copy-start | bytes 1540
  13.0 99.9 %all-to-all-start = ((bf16[4,256,4096]{2,1,0:T(8,128)(2,1)}), bf16[4,256,4096]{2,1,0:T(8,128)(2,1)}, u32[]{:S(2)}, u32[]{:S(2)}) async-start(bf16[4,256,4096]{2,1,0:T(8,128)(2,1)} %stack.2), calls=%async_computation | async-start | bytes 16777216 | tf_op jit(solution)/shard_map/all_to_all | solution.py:35
  18.8 224.9 %reduce-scatter.3.cloned.1.call-start = ((), (), s32[]{:S(2)}) async-start(), calls=%async_computation.3 | async-start | bytes 4456448 | tf_op jit(solution)/shard_map/reduce_scatter | solution.py:61
  121.3 52.2 %copy-start.1 = (s32[512]{0:T(512)S(1)}, s32[512]{0:T(512)}, u32[]{:S(2)}) copy-start(s32[512]{0:T(512)} %param.7) | copy-start | bytes 6148
  183.8 153.5 %reduce-scatter.5.cloned.1.call-start = ((), (), s32[]{:S(2)}) async-start(), calls=%async_computation.4 | async-start | bytes 8912896 | tf_op jit(solution)/shard_map/reduce_scatter | solution.py:66
Sparse Core Ops, SparseCore 0:
  184.0 59.7 reduce-scatter.2
  248.0 89.2 reduce-scatter.4
